TPU v7x, 32 devices: a whole 2x2x4 slice. The times are simulated.
32 devices in a mesh: dp: 8 (over y, x, core), seq: 4 (over z).
Axes of the slice: x: 2, y: 2, z: 4, core: 2. Of those that a mesh axis runs over, the one named last changes fastest.
Arguments:
- block_input: float32 [32, 200, 768], P(('dp', 'seq')), may hold values from -6 to 6
- norm1_gain: bfloat16 [768], P('dp'), may hold values from 0.5 to 1.5
- norm1_bias: bfloat16 [768], P('dp'), may hold values from -1 to 1
- qkv_weight: bfloat16 [768, 2304], P('dp'), may hold values from -0.21875 to 0.21875
- query_bias: bfloat16 [768], P('dp'), may hold values from -1 to 1
- value_bias: bfloat16 [768], P('dp'), may hold values from -1 to 1
- out_weight: bfloat16 [768, 768], P('dp'), may hold values from -0.875 to 0.875
- out_bias: bfloat16 [768], P('dp'), may hold values from -1 to 1
- norm2_gain: bfloat16 [768], P('dp'), may hold values from 0.5 to 1.5
- norm2_bias: bfloat16 [768], P('dp'), may hold values from -1 to 1
- router_weight: bfloat16 [768, 32], P('dp'), may hold values from -0.21875 to 0.21875
- gate_weight: bfloat16 [32, 768, 2048], P('dp', None, 'seq'), may hold values from -0.21875 to 0.21875
- up_weight: bfloat16 [32, 768, 2048], P('dp', None, 'seq'), may hold values from -0.21875 to 0.21875
- down_weight: bfloat16 [32, 2048, 768], P('dp', 'seq'), may hold values from -2 to 2
- routes: int32 [32, 200, 2], P(('dp', 'seq')), may hold values from 0 to 31, all different within a row; in each aligned block of 200 rows (0 to 199, 200 to 399, ..., all dimensions but the last counted through in order) at most 14 rows name the same one
- key_mask: int32 [32, 200], P('dp'), may hold values from 0 to 1, as said below
- cotangent: float32 [32, 200, 768], P(('dp', 'seq')), may hold values from -6 to 6
Outputs:
- block_output: float32 [32, 200, 768], P(('dp', 'seq'))
- input_grad: float32 [32, 200, 768], P(('dp', 'seq'))
- norm1_gain_grad: float32 [768], P('dp')
- norm1_bias_grad: float32 [768], P('dp')
- qkv_weight_grad: float32 [768, 2304], P('dp')
- query_bias_grad: float32 [768], P('dp')
- value_bias_grad: float32 [768], P('dp')
- out_weight_grad: float32 [768, 768], P('dp')
- out_bias_grad: float32 [768], P('dp')
- norm2_gain_grad: float32 [768], P('dp')
- norm2_bias_grad: float32 [768], P('dp')
- router_weight_grad: float32 [768, 32], P('dp')
- gate_weight_grad: float32 [32, 768, 2048], P('dp', None, 'seq')
- up_weight_grad: float32 [32, 768, 2048], P('dp', None, 'seq')
- down_weight_grad: float32 [32, 2048, 768], P('dp', 'seq')
Inputs may be any that keep to these rules, and one draw needn't show every extreme that they name: `routes`: in each image, no expert is named by more than 14 tokens; a token's 2 experts differ. `key_mask`: each image has exactly 3 zeros, at positions that differ from image to image.
All inputs are finite; a program needn't handle non-finite values.
Results may differ from a plain program's by a relative error of at most 0.028.
Values may be sent and summed in bfloat16 or wider, within the bound.
No kernel may reach another device: no remote copies, remote signals or barrier semaphores. Data moves between devices by JAX's collectives and lax.ppermute only.
A program may use at most 192 MiB of HBM per device.

v0:
```python
import math
import jax
import jax.numpy as jnp
from jax import lax
from jax.sharding import PartitionSpec as P

HEAD = 64
EXPERTS = 32
TOP = 2
CAP = 14
epsilon = 1e-06


def normalize(values, norm_gain, norm_bias):
    average = jnp.mean(values, axis=-1, keepdims=True)
    centred = values - average
    variance = jnp.mean(centred * centred, axis=-1, keepdims=True)
    inverse = lax.rsqrt(variance + epsilon)
    unit_rows = centred * inverse
    scaled = unit_rows * norm_gain.astype(jnp.float32) + norm_bias.astype(jnp.float32)
    return (scaled, unit_rows, inverse)


def normalize_back(upstream, unit_rows, inverse, norm_gain):
    scaled = upstream * norm_gain.astype(jnp.float32)
    mean_term = jnp.mean(scaled, axis=-1, keepdims=True)
    proj_term = jnp.mean(scaled * unit_rows, axis=-1, keepdims=True)
    return inverse * (scaled - mean_term - unit_rows * proj_term)


def gelu_tanh(values):
    return jax.nn.gelu(values, approximate=True)


def to_heads(tensor):
    return lax.all_to_all(tensor, "seq", split_axis=2, concat_axis=0, tiled=True)


def to_tokens(tensor):
    return lax.all_to_all(tensor, "seq", split_axis=0, concat_axis=1, tiled=True)


def to_owners(tensor):
    return lax.all_to_all(tensor, "dp", split_axis=0, concat_axis=1, tiled=True)


def to_sources(tensor):
    return lax.all_to_all(tensor, "dp", split_axis=1, concat_axis=0, tiled=True)


def gather_rows(tensor):
    return lax.all_gather(tensor, "seq", axis=1, tiled=True)


def sum_partial(tensor):
    return lax.psum_scatter(
        tensor.astype(jnp.bfloat16), "seq", scatter_dimension=1, tiled=True
    ).astype(jnp.float32)


def compute_scores(head_q, head_k):
    scores = jnp.einsum("ihdq,ihdk->ihqk", head_q, head_k, preferred_element_type=jnp.float32)
    return scores * (1.0 / math.sqrt(HEAD))


def fill_slots(place_list, value_list):
    images = value_list[0].shape[0]
    width = value_list[0].shape[2]
    total = jnp.einsum(
        "sx,sd->xd", place_list[0][0], value_list[0][0], preferred_element_type=jnp.float32
    )
    for route_index in range(1, len(place_list)):
        total = total + jnp.einsum(
            "sx,sd->xd",
            place_list[route_index][0],
            value_list[route_index][0],
            preferred_element_type=jnp.float32,
        )
    per_image = [total.reshape(EXPERTS, CAP, width)]
    return jnp.stack(per_image, axis=1).astype(jnp.bfloat16).reshape(EXPERTS, images * CAP, width)


def read_slots(place_rows, returned, split_count):
    images = place_rows.shape[0]
    width = returned.shape[-1]
    shaped = returned.reshape(EXPERTS, split_count, images, CAP, width)
    total = jnp.dot(
        place_rows[0],
        shaped[:, 0, 0].reshape(EXPERTS * CAP, width),
        preferred_element_type=jnp.float32,
    )
    for half_index in range(1, split_count):
        total = total + jnp.dot(
            place_rows[0],
            shaped[:, half_index, 0].reshape(EXPERTS * CAP, width),
            preferred_element_type=jnp.float32,
        )
    per_image = [total]
    return jnp.stack(per_image, axis=0)


def per_device(
    block_input,
    norm1_gain,
    norm1_bias,
    qkv_weight,
    query_bias,
    value_bias,
    out_weight,
    out_bias,
    norm2_gain,
    norm2_bias,
    router_weight,
    gate_weight,
    up_weight,
    down_weight,
    routes,
    key_mask,
    cotangent,
):
    images, seq_rows, model_width = block_input.shape
    groups = lax.axis_size("seq")
    owners = lax.axis_size("dp")
    split_count = max(1, owners // EXPERTS)
    group_width = model_width // groups
    head_count = group_width // HEAD
    all_images = images * groups
    (
        gain_one,
        shift_one,
        qkv_full,
        query_full,
        value_full,
        out_full,
        obias_full,
        gain_two,
        shift_two,
        router_full,
    ) = (
        lax.all_gather(norm1_gain, "dp", axis=0, tiled=True),
        lax.all_gather(norm1_bias, "dp", axis=0, tiled=True),
        lax.all_gather(qkv_weight, "dp", axis=0, tiled=True),
        lax.all_gather(query_bias, "dp", axis=0, tiled=True),
        lax.all_gather(value_bias, "dp", axis=0, tiled=True),
        lax.all_gather(out_weight, "dp", axis=0, tiled=True),
        lax.all_gather(out_bias, "dp", axis=0, tiled=True),
        lax.all_gather(norm2_gain, "dp", axis=0, tiled=True),
        lax.all_gather(norm2_bias, "dp", axis=0, tiled=True),
        lax.all_gather(router_weight, "dp", axis=0, tiled=True),
    )
    normed_one, unit_one, inverse_one = normalize(block_input, gain_one, shift_one)
    normed_one = normed_one.astype(jnp.bfloat16)
    bias_row = jnp.concatenate(
        [
            query_full.astype(jnp.float32),
            jnp.zeros((model_width,), jnp.float32),
            value_full.astype(jnp.float32),
        ]
    )
    projected = (
        jnp.einsum("isd,df->ifs", normed_one, qkv_full, preferred_element_type=jnp.float32)
        + bias_row[None, :, None]
    ).astype(jnp.bfloat16)
    packed = projected.reshape(images, 3, groups, group_width, seq_rows)
    qkv_heads = to_heads(packed)
    head_q = qkv_heads[:, 0, 0].reshape(all_images, head_count, HEAD, seq_rows)
    head_k = qkv_heads[:, 1, 0].reshape(all_images, head_count, HEAD, seq_rows)
    head_v = qkv_heads[:, 2, 0].reshape(all_images, head_count, HEAD, seq_rows)
    key_open = key_mask.astype(jnp.float32)[:, None, None, :]
    scores = compute_scores(head_q, head_k)
    log_total = jnp.log(jnp.sum(jnp.exp(scores) * key_open, axis=-1))
    probs_b = (jnp.exp(scores - log_total[..., None]) * key_open).astype(jnp.bfloat16)
    mixed_heads = jnp.einsum("ihqk,ihdk->ihdq", probs_b, head_v, preferred_element_type=jnp.float32)
    mixed = to_tokens(mixed_heads.astype(jnp.bfloat16).reshape(all_images, group_width, seq_rows))
    residual_one = (
        block_input
        + jnp.einsum("ids,de->ise", mixed, out_full, preferred_element_type=jnp.float32)
        + obias_full.astype(jnp.float32)
    )
    normed_two, unit_two, inverse_two = normalize(residual_one, gain_two, shift_two)
    normed_two = normed_two.astype(jnp.bfloat16)
    logits = jnp.dot(normed_two, router_full, preferred_element_type=jnp.float32)
    expert_ids = jnp.arange(EXPERTS, dtype=jnp.int32)
    route_hot = (routes[..., None] == expert_ids).astype(jnp.int32)
    route_float = route_hot.astype(jnp.float32)
    logit_exp = jnp.exp(logits)
    router_probs = logit_exp / jnp.sum(logit_exp, axis=-1, keepdims=True)
    per_token = jnp.sum(route_hot, axis=2)
    earlier = jnp.cumsum(per_token, axis=1) - per_token
    slots = jnp.sum(route_hot * earlier[:, :, None, :], axis=-1)
    slot_ids = jnp.arange(EXPERTS * CAP, dtype=jnp.int32)
    places = []
    gates = []
    for route_index in range(TOP):
        target = routes[:, :, route_index] * CAP + slots[:, :, route_index]
        places.append((target[..., None] == slot_ids).astype(jnp.bfloat16))
        gates.append(jnp.sum(route_float[:, :, route_index] * router_probs, axis=-1))
    place_all = places[0]
    route_index = 1
    place_all = place_all + places[route_index]
    send_rows = fill_slots([place_all], [normed_two])
    send_rows = jnp.repeat(send_rows, split_count, axis=0)
    arrived = to_owners(send_rows)
    rows_all = gather_rows(arrived)
    gate_use, up_use, down_use = (gate_weight, up_weight, down_weight)
    gate_pre = jnp.einsum("prd,pdf->prf", rows_all, gate_use, preferred_element_type=jnp.float32)
    up_pre = jnp.einsum("prd,pdf->prf", rows_all, up_use, preferred_element_type=jnp.float32)
    activated, gelu_back = jax.vjp(gelu_tanh, gate_pre)
    hidden = (activated * up_pre).astype(jnp.bfloat16)
    partial_out = jnp.einsum("prf,pfd->prd", hidden, down_use, preferred_element_type=jnp.float32)
    piece_out = sum_partial(partial_out).astype(jnp.bfloat16)
    returned = to_sources(piece_out)
    expert_outs = [
        read_slots(places[route_index], returned, split_count) for route_index in range(TOP)
    ]
    block_output = residual_one
    for route_index in range(TOP):
        block_output = block_output + gates[route_index][..., None] * expert_outs[route_index]
    gate_grads = [
        jnp.sum(cotangent * expert_outs[route_index], axis=-1) for route_index in range(TOP)
    ]
    routed_grads = [
        (gates[route_index][..., None] * cotangent).astype(jnp.bfloat16)
        for route_index in range(TOP)
    ]
    send_grad = fill_slots(places, routed_grads)
    send_grad = jnp.repeat(send_grad, split_count, axis=0)
    arrived_grad = to_owners(send_grad)
    rows_grad = gather_rows(arrived_grad)
    hidden_grad = jnp.einsum(
        "prd,pfd->prf", rows_grad, down_use, preferred_element_type=jnp.float32
    )
    down_grad = jnp.einsum("prf,prd->pfd", hidden, rows_grad, preferred_element_type=jnp.float32)
    gate_pre_grad = gelu_back(hidden_grad * up_pre)[0].astype(jnp.bfloat16)
    up_pre_grad = (hidden_grad * activated).astype(jnp.bfloat16)
    gate_grad_w = jnp.einsum(
        "prd,prf->pdf", rows_all, gate_pre_grad, preferred_element_type=jnp.float32
    )
    up_grad_w = jnp.einsum(
        "prd,prf->pdf", rows_all, up_pre_grad, preferred_element_type=jnp.float32
    )
    rows_back = jnp.einsum(
        "prf,pdf->prd", gate_pre_grad, gate_use, preferred_element_type=jnp.float32
    ) + jnp.einsum("prf,pdf->prd", up_pre_grad, up_use, preferred_element_type=jnp.float32)
    rows_back = sum_partial(rows_back).astype(jnp.bfloat16)
    back_grad = to_sources(rows_back)
    moe_grad = read_slots(place_all, back_grad, split_count)
    spread = route_float[:, :, 0] * gate_grads[0][..., None]
    route_index = 1
    spread = spread + route_float[:, :, route_index] * gate_grads[route_index][..., None]
    logit_grad = (
        router_probs * (spread - jnp.sum(router_probs * spread, axis=-1, keepdims=True))
    ).astype(jnp.bfloat16)
    router_grad = jnp.einsum(
        "isd,ise->de", normed_two, logit_grad, preferred_element_type=jnp.float32
    )
    normed_two_grad = moe_grad + jnp.dot(
        logit_grad, router_full.T, preferred_element_type=jnp.float32
    )
    gain_two_grad = jnp.sum(normed_two_grad * unit_two, axis=(0, 1))
    shift_two_grad = jnp.sum(normed_two_grad, axis=(0, 1))
    residual_grad = cotangent + normalize_back(normed_two_grad, unit_two, inverse_two, gain_two)
    residual_b = residual_grad.astype(jnp.bfloat16)
    out_weight_grad = jnp.einsum(
        "ids,ise->de", mixed, residual_b, preferred_element_type=jnp.float32
    )
    out_bias_grad = jnp.sum(residual_grad, axis=(0, 1))
    mixed_grad = jnp.einsum(
        "ise,de->ids", residual_b, out_full, preferred_element_type=jnp.float32
    ).astype(jnp.bfloat16)
    mixed_grad = to_heads(mixed_grad.reshape(images, 1, groups, group_width, seq_rows))
    grad_heads = mixed_grad[:, 0, 0].reshape(all_images, head_count, HEAD, seq_rows)
    probs = jnp.exp(compute_scores(head_q, head_k) - log_total[..., None]) * key_open
    probs_grad = jnp.einsum(
        "ihdq,ihdk->ihqk", grad_heads, head_v, preferred_element_type=jnp.float32
    )
    row_term = jnp.sum(probs * probs_grad, axis=-1, keepdims=True)
    score_grad = (probs * (probs_grad - row_term) * (1.0 / math.sqrt(HEAD))).astype(jnp.bfloat16)
    value_grad = jnp.einsum(
        "ihqk,ihdq->ihdk", probs_b, grad_heads, preferred_element_type=jnp.float32
    ).astype(jnp.bfloat16)
    query_grad = jnp.einsum(
        "ihqk,ihdk->ihdq", score_grad, head_k, preferred_element_type=jnp.float32
    ).astype(jnp.bfloat16)
    key_grad = jnp.einsum(
        "ihqk,ihdq->ihdk", score_grad, head_q, preferred_element_type=jnp.float32
    ).astype(jnp.bfloat16)
    packed_grad = jnp.stack(
        [
            query_grad.reshape(all_images, group_width, seq_rows),
            key_grad.reshape(all_images, group_width, seq_rows),
            value_grad.reshape(all_images, group_width, seq_rows),
        ],
        axis=1,
    )
    tokens_grad = to_tokens(packed_grad.reshape(all_images, 3 * group_width, seq_rows))
    grouped_grad = tokens_grad.reshape(images, groups, 3, group_width, seq_rows)
    qkv_weight_grad = jnp.einsum(
        "isd,igtcs->dtgc", normed_one, grouped_grad, preferred_element_type=jnp.float32
    ).reshape(model_width, 3 * model_width)
    query_bias_grad = jnp.sum(grouped_grad[:, :, 0].astype(jnp.float32), axis=(0, 3)).reshape(
        model_width
    )
    value_bias_grad = jnp.sum(grouped_grad[:, :, 2].astype(jnp.float32), axis=(0, 3)).reshape(
        model_width
    )
    qkv_grouped = qkv_full.reshape(model_width, 3, groups, group_width)
    normed_one_grad = jnp.einsum(
        "igtcs,dtgc->isd", grouped_grad, qkv_grouped, preferred_element_type=jnp.float32
    )
    gain_one_grad = jnp.sum(normed_one_grad * unit_one, axis=(0, 1))
    shift_one_grad = jnp.sum(normed_one_grad, axis=(0, 1))
    input_grad = residual_grad + normalize_back(normed_one_grad, unit_one, inverse_one, gain_one)
    shares = (
        lax.psum_scatter(gain_one_grad, "dp", scatter_dimension=0, tiled=True),
        lax.psum_scatter(shift_one_grad, "dp", scatter_dimension=0, tiled=True),
        lax.psum_scatter(qkv_weight_grad, "dp", scatter_dimension=0, tiled=True),
        lax.psum_scatter(query_bias_grad, "dp", scatter_dimension=0, tiled=True),
        lax.psum_scatter(value_bias_grad, "dp", scatter_dimension=0, tiled=True),
        lax.psum_scatter(out_weight_grad, "dp", scatter_dimension=0, tiled=True),
        lax.psum_scatter(out_bias_grad, "dp", scatter_dimension=0, tiled=True),
        lax.psum_scatter(gain_two_grad, "dp", scatter_dimension=0, tiled=True),
        lax.psum_scatter(shift_two_grad, "dp", scatter_dimension=0, tiled=True),
        lax.psum_scatter(router_grad, "dp", scatter_dimension=0, tiled=True),
    )
    (
        gain_one_sum,
        shift_one_sum,
        qkv_sum,
        query_sum,
        value_sum,
        out_sum,
        obias_sum,
        gain_two_sum,
        shift_two_sum,
        router_sum,
    ) = (
        lax.psum(shares[0].astype(jnp.bfloat16), "seq").astype(jnp.float32),
        lax.psum(shares[1].astype(jnp.bfloat16), "seq").astype(jnp.float32),
        lax.psum(shares[2].astype(jnp.bfloat16), "seq").astype(jnp.float32),
        lax.psum(shares[3].astype(jnp.bfloat16), "seq").astype(jnp.float32),
        lax.psum(shares[4].astype(jnp.bfloat16), "seq").astype(jnp.float32),
        lax.psum(shares[5].astype(jnp.bfloat16), "seq").astype(jnp.float32),
        lax.psum(shares[6].astype(jnp.bfloat16), "seq").astype(jnp.float32),
        lax.psum(shares[7].astype(jnp.bfloat16), "seq").astype(jnp.float32),
        lax.psum(shares[8].astype(jnp.bfloat16), "seq").astype(jnp.float32),
        lax.psum(shares[9].astype(jnp.bfloat16), "seq").astype(jnp.float32),
    )
    return (
        block_output,
        input_grad,
        gain_one_sum,
        shift_one_sum,
        qkv_sum,
        query_sum,
        value_sum,
        out_sum,
        obias_sum,
        gain_two_sum,
        shift_two_sum,
        router_sum,
        gate_grad_w,
        up_grad_w,
        down_grad,
    )


def solution(mesh):
    in_specs = (
        P(("dp", "seq"), None, None),
        P("dp"),
        P("dp"),
        P("dp", None),
        P("dp"),
        P("dp"),
        P("dp", None),
        P("dp"),
        P("dp"),
        P("dp"),
        P("dp", None),
        P("dp", None, "seq"),
        P("dp", None, "seq"),
        P("dp", "seq", None),
        P(("dp", "seq"), None, None),
        P("dp", None),
        P(("dp", "seq"), None, None),
    )
    out_specs = (
        P(("dp", "seq"), None, None),
        P(("dp", "seq"), None, None),
        P("dp"),
        P("dp"),
        P("dp", None),
        P("dp"),
        P("dp"),
        P("dp", None),
        P("dp"),
        P("dp"),
        P("dp"),
        P("dp", None),
        P("dp", None, "seq"),
        P("dp", None, "seq"),
        P("dp", "seq", None),
    )
    return jax.shard_map(
        per_device, mesh=mesh, in_specs=in_specs, out_specs=out_specs, check_vma=False
    )
```

profile of v0, /device:TPU:0, one launch (start us, length us, event | category | flops | bytes accessed | tf_op | source)
XLA Modules:
  0.0 666.3 jit_solution(9371943102563862651)
XLA Ops:
  15.9 26.9 %all-reduce.16 = (bf16[768]{0:T(1024)(128)(2,1)S(1)}, bf16[768]{0:T(1024)(128)(2,1)S(1)}, bf16[768]{0:T(1024)(128)(2,1)S(1)}, bf16[768]{0:T(1024)(128)(2,1)S(1)}...) all-reduce(bf16[768]{0:T(1024)(128)(2,1)S(1)} %dynamic-update-slice, ...), channel_id=1, replica_groups=mesh['dp'=8,'seq'=4] {'dp'}, use_global_device_ids=true, to_apply=%add.4 | all-reduce | flops 5376 | bytes 21504
  46.7 4.1 fusion.10
  58.0 4.6 all-to-all-start
  65.8 25.9 %all-to-all-done = bf16[1,3,4,192,200]{4,3,1,0,2:T(8,128)(2,1)} async-done(((bf16[1,3,4,192,200]{4,3,1,0,2:T(8,128)(2,1)}), bf16[1,3,4,192,200]{4,3,1,0,2:T(8,128)(2,1)}, u32[]{:S(2)}, u32[]{:S(2)}) %all-to-all-start) | async-done | bytes 921632 | tf_op jit(solution)/shard_map/all_to_all | solution.py:36
  95.7 4.3 convolution_convert_fusion.3
  108.2 6.5 all-to-all-done.1
  118.7 15.0 %all_to_all.111 = bf16[32,14,768]{2,1,0:T(8,128)(2,1)S(1)} all-to-all(bf16[32,14,768]{2,1,0:T(8,128)(2,1)S(1)} %copy.104), channel_id=1, replica_groups=mesh['dp'=8,'seq'=4] {'dp'}, dimensions={0} | all-to-all | bytes 1376256 | tf_op jit(solution)/shard_map/all_to_all | solution.py:44
  135.3 54.0 %all-gather.10.cloned.1.call-done = bf16[4,448,768]{2,1,0:T(8,128)(2,1)} async-done(((bf16[4,112,768]{2,1,0:T(8,128)(2,1)}), bf16[4,448,768]{2,1,0:T(8,128)(2,1)}) %all-gather.10.cloned.1.call-update) | async-done | bytes 2752528 | tf_op jit(solution)/shard_map/all_gather | solution.py:52
  189.3 4.5 fusion.128
  193.8 3.8 multiply_convert_fusion.1
  202.0 53.2 %reduce-scatter.10.cloned.1.call-done = bf16[4,112,768]{2,1,0:T(8,128)(2,1)} async-done(((bf16[4,448,768]{2,1,0:T(8,128)(2,1)}), bf16[4,112,768]{2,1,0:T(8,128)(2,1)}) %reduce-scatter.10.cloned.1.call-update) | async-done | bytes 688144 | tf_op jit(solution)/shard_map/reduce_scatter | solution.py:56
  257.5 4.2 all-to-all-start.3
  261.8 14.8 %all-gather = bf16[8,96,32]{1,2,0:T(8,128)(2,1)S(1)} all-gather(bf16[1,96,32]{1,2,0:T(8,128)(2,1)} %bitcast.285), channel_id=1, replica_groups=mesh['dp'=8,'seq'=4] {'dp'}, dimensions={0}, use_global_device_ids=true | all-gather | bytes 55296 | tf_op jit(solution)/shard_map/all_gather | solution.py:149
  295.5 16.0 %all_to_all.112 = bf16[32,14,768]{2,1,0:T(8,128)(2,1)S(1)} all-to-all(bf16[32,14,768]{2,1,0:T(8,128)(2,1)} %convert_element_type.299), channel_id=1, replica_groups=mesh['dp'=8,'seq'=4] {'dp'}, dimensions={0} | all-to-all | bytes 1376256 | tf_op jit(solution)/shard_map/all_to_all | solution.py:44
  313.3 54.3 %all-gather.12.cloned.1.call-done = bf16[4,448,768]{2,1,0:T(8,128)(2,1)} async-done(((bf16[4,112,768]{2,1,0:T(8,128)(2,1)}), bf16[4,448,768]{2,1,0:T(8,128)(2,1)}) %all-gather.12.cloned.1.call-update) | async-done | bytes 2752528 | tf_op jit(solution)/shard_map/all_gather | solution.py:52
  367.7 7.1 %multiply_convert_fusion = (bf16[4,448,512]{2,1,0:T(8,128)(2,1)S(1)}, bf16[4,448,512]{2,1,0:T(8,128)(2,1)S(1)}) fusion(f32[4,448,512]{2,1,0:T(8,128)} %copy-done.23, f32[4,448,512]{2,1,0:T(8,128)} %get-tuple-element.114, bf16[4,448,768]{2,1,0:T(8,128)(2,1)} %all-gather.12.cloned.1.call-done, bf16[4,512,768]{2,1,0:T(8,128)(2,1)S(1)} %copy-done), kind=kOutput, calls=%fused_computation.14 | convolution fusion | flops 1431306240 | bytes 16908288 | tf_op jit(solution)/shard_map/prd,pfd->prf/dot_general | solution.py:230
  381.4 53.2 %reduce-scatter.12.cloned.1.call-done = bf16[4,112,768]{2,1,0:T(8,128)(2,1)} async-done(((bf16[4,448,768]{2,1,0:T(8,128)(2,1)}), bf16[4,112,768]{2,1,0:T(8,128)(2,1)}) %reduce-scatter.12.cloned.1.call-update) | async-done | bytes 688144 | tf_op jit(solution)/shard_map/reduce_scatter | solution.py:56
  442.9 9.0 %all-to-all-done.5 = bf16[4,112,768]{2,0,1:T(4,128)(2,1)S(1)} async-done(((bf16[4,112,768]{2,0,1:T(4,128)(2,1)}), bf16[4,112,768]{2,0,1:T(4,128)(2,1)S(1)}, u32[]{:S(2)}, u32[]{:S(2)}) %all-to-all-start.5) | async-done | bytes 688160 | tf_op jit(solution)/shard_map/all_to_all | solution.py:48
  470.2 6.1 all-to-all-done.6
  477.0 4.3 convolution_convert_fusion.2
  483.0 4.0 fusion.33
  486.9 4.2 fusion.30
  493.3 26.0 %all_to_all.113 = bf16[4,576,200]{1,2,0:T(8,128)(2,1)} all-to-all(bf16[4,576,200]{1,2,0:T(8,128)(2,1)S(1)} %copy.120), channel_id=1, replica_groups=mesh['dp'=8,'seq'=4] {'seq'}, dimensions={0} | all-to-all | bytes 1843200 | tf_op jit(solution)/shard_map/all_to_all | solution.py:40
  525.5 8.0 %copy.134 = f32[768,2304]{1,0:T(8,128)} copy(f32[768,2304]{0,1:T(8,128)} %bitcast.243) | data formatting | bytes 14155776
  534.5 5.9 copy.122
  541.3 6.8 %fusion.132 = f32[4,768,512]{2,1,0:T(8,128)} fusion(bf16[4,448,768]{2,1,0:T(8,128)(2,1)S(1)} %copy-done.3, bf16[4,448,512]{2,1,0:T(8,128)(2,1)} %copy-done.16), kind=kOutput, calls=%fused_computation.185 | convolution fusion | flops 1409286144 | bytes 10878976 | tf_op jit(solution)/shard_map/prd,prf->pdf/dot_general | solution.py:236
  548.0 4.6 fusion.133
  552.6 4.6 fusion.134
  557.8 3.8 fusion.43
  563.3 38.4 %reduce-scatter.16.cloned.1.call-done = f32[96,2304]{1,0:T(8,128)} async-done(((f32[768,2304]{1,0:T(8,128)}), f32[96,2304]{1,0:T(8,128)}) %reduce-scatter.16.cloned.1.call-update) | async-done | bytes 884752
  605.3 23.7 %all-reduce.15 = (bf16[768]{0:T(1024)(128)(2,1)S(1)}, bf16[768]{0:T(1024)(128)(2,1)S(1)}, bf16[768]{0:T(1024)(128)(2,1)S(1)}, bf16[768]{0:T(1024)(128)(2,1)S(1)}...) all-reduce(f32[768]{0:T(1024)S(1)} %get-tuple-element.62, ...), channel_id=4, replica_groups=mesh['dp'=8,'seq'=4] {'dp'}, use_global_device_ids=true, to_apply=%region_23.24.clone | all-reduce | flops 5376 | bytes 32256
  629.6 19.1 %all-reduce.17 = (bf16[96]{0:T(256)(128)(2,1)S(1)}, bf16[96]{0:T(256)(128)(2,1)S(1)}, bf16[96]{0:T(256)(128)(2,1)S(1)}, bf16[96]{0:T(256)(128)(2,1)S(1)}, bf16[9...) all-reduce(bf16[96]{0:T(256)(128)(2,1)S(1)} %dynamic-slice.34, ...), channel_id=1, replica_groups=mesh['dp'=8,'seq'=4] {'seq'}, use_global_device_ids=true, to_apply=%region_24.25 | all-reduce | flops 3744 | bytes 14976 | tf_op jit(solution)/shard_map/psum | solution.py:338
  (305 shorter events, 128.9 us)
Async XLA Ops:
  7.2 191.7 %copy-start = (bf16[4,512,768]{2,1,0:T(8,128)(2,1)S(1)}, bf16[4,512,768]{2,1,0:T(8,128)(2,1)}, u32[]{:S(2)}) copy-start(bf16[4,512,768]{2,1,0:T(8,128)(2,1)} %param.30) | copy-start | bytes 9437188
  7.2 39.5 %all-gather.6.cloned.1.call-start = ((), (), s32[]{:S(2)}) async-start(), calls=%async_computation.13 | async-start | bytes 3981312 | tf_op jit(solution)/shard_map/all_gather | solution.py:142
  58.0 33.6 %all-to-all-start = ((bf16[1,3,4,192,200]{4,3,1,0,2:T(8,128)(2,1)}), bf16[1,3,4,192,200]{4,3,1,0,2:T(8,128)(2,1)}, u32[]{:S(2)}, u32[]{:S(2)}) async-start(bf16[1,3,4,192,200]{4,3,1,0,2:T(8,128)(2,1)} %copy.98), calls=%async_computation | async-start | bytes 2359296 | tf_op jit(solution)/shard_map/all_to_all | solution.py:36
  62.6 45.6 %all-gather.8.cloned.1.call-start = ((), (), s32[]{:S(2)}) async-start(), calls=%async_computation.14 | async-start | bytes 1327104 | tf_op jit(solution)/shard_map/all_gather | solution.py:145
  64.0 31.7 %copy-start.73 = (f32[4,200]{1,0:T(4,128)}, f32[4,200]{1,0:T(4,128)S(1)}, u32[]{:S(2)}) copy-start(f32[4,200]{1,0:T(4,128)S(1)} %convert_element_type.280) | copy-start | bytes 9604
  100.0 14.7 %all-to-all-start.1 = ((bf16[4,192,200]{2,1,0:T(8,128)(2,1)}), bf16[4,192,200]{2,1,0:T(8,128)(2,1)S(1)}, u32[]{:S(2)}, u32[]{:S(2)}) async-start(bf16[4,192,200]{2,1,0:T(8,128)(2,1)} %bitcast.269), calls=%async_computation.1 | async-start | bytes 786432 | tf_op jit(solution)/shard_map/all_to_all | solution.py:40
  103.5 85.8 %all-gather.10.cloned.1.call-start = ((), (), s32[]{:S(2)}) async-start(), calls=%async_computation.15 | async-start | bytes 3440640 | tf_op jit(solution)/shard_map/all_gather | solution.py:52
  135.0 120.2 %reduce-scatter.10.cloned.1.call-start = ((), (), s32[]{:S(2)}) async-start(), calls=%async_computation.16 | async-start | bytes 3440640 | tf_op jit(solution)/shard_map/reduce_scatter | solution.py:56
  257.5 24.3 %all-to-all-start.3 = ((bf16[4,112,768]{2,0,1:T(4,128)(2,1)}), bf16[4,112,768]{2,0,1:T(4,128)(2,1)}, u32[]{:S(2)}, u32[]{:S(2)}) async-start(bf16[4,112,768]{2,0,1:T(4,128)(2,1)} %copy.107), calls=%async_computation.4 | async-start | bytes 1376256 | tf_op jit(solution)/shard_map/all_to_all | solution.py:48
  261.7 106.0 %all-gather.12.cloned.1.call-start = ((), (), s32[]{:S(2)}) async-start(), calls=%async_computation.17 | async-start | bytes 3440640 | tf_op jit(solution)/shard_map/all_gather | solution.py:52
  312.8 121.8 %reduce-scatter.12.cloned.1.call-start = ((), (), s32[]{:S(2)}) async-start(), calls=%async_computation.18 | async-start | bytes 3440640 | tf_op jit(solution)/shard_map/reduce_scatter | solution.py:56
  381.3 59.3 %copy-start.36 = (f32[1,200,2,32]{1,3,2,0:T(8,128)S(1)}, f32[1,200,2,32]{1,3,2,0:T(8,128)}, u32[]{:S(2)}) copy-start(f32[1,200,2,32]{1,3,2,0:T(8,128)} %convert_convert_fusion) | copy-start | bytes 153604
  381.3 59.3 %copy-start.40 = (f32[200,32]{0,1:T(8,128)S(1)}, f32[200,32]{0,1:T(8,128)}, u32[]{:S(2)}) copy-start(f32[200,32]{0,1:T(8,128)} %get-tuple-element.117) | copy-start | bytes 76804
  381.3 59.3 %copy-start.66 = (f32[200]{0:T(256)S(1)}, f32[200]{0:T(256)}, u32[]{:S(2)}) copy-start(f32[200]{0:T(256)} %get-tuple-element.116) | copy-start | bytes 2404
  381.3 59.3 %copy-start.68 = (f32[200]{0:T(256)S(1)}, f32[200]{0:T(256)}, u32[]{:S(2)}) copy-start(f32[200]{0:T(256)} %copy-done.67) | copy-start | bytes 2404
  381.3 59.3 %copy-start.70 = (f32[200]{0:T(256)S(1)}, f32[200]{0:T(256)}, u32[]{:S(2)}) copy-start(f32[200]{0:T(256)} %copy-done.69) | copy-start | bytes 2404
  381.3 59.3 %copy-start.75 = (f32[200]{0:T(256)S(1)}, f32[200]{0:T(256)}, u32[]{:S(2)}) copy-start(f32[200]{0:T(256)} %get-tuple-element.72) | copy-start | bytes 2404
  381.3 59.3 %copy-start.27 = (bf16[1,200,768]{2,1,0:T(8,128)(2,1)S(1)}, bf16[1,200,768]{2,1,0:T(8,128)(2,1)}, u32[]{:S(2)}) copy-start(bf16[1,200,768]{2,1,0:T(8,128)(2,1)} %copy-done.26) | copy-start | bytes 921604
  381.4 60.5 %copy-start.37 = (bf16[768,32]{0,1:T(8,128)(2,1)S(1)}, bf16[768,32]{0,1:T(8,128)(2,1)}, u32[]{:S(2)}) copy-start(bf16[768,32]{0,1:T(8,128)(2,1)} %reshape.675) | copy-start | bytes 147460
  436.8 15.1 %all-to-all-start.5 = ((bf16[4,112,768]{2,0,1:T(4,128)(2,1)}), bf16[4,112,768]{2,0,1:T(4,128)(2,1)S(1)}, u32[]{:S(2)}, u32[]{:S(2)}) async-start(bf16[4,112,768]{2,0,1:T(4,128)(2,1)} %copy.111), calls=%async_computation.7 | async-start | bytes 1376256 | tf_op jit(solution)/shard_map/all_to_all | solution.py:48
  440.5 99.9 %reduce-scatter.18.cloned.1.call-start = ((), (), s32[]{:S(2)}) async-start(), calls=%async_computation.21 | async-start | bytes 442368
  441.8 119.8 %reduce-scatter.14.cloned.1.call-start = ((), (), s32[]{:S(2)}) async-start(), calls=%async_computation.19 | async-start | bytes 2654208 | tf_op jit(solution)/shard_map/reduce_scatter | solution.py:320
  463.6 12.6 %all-to-all-start.6 = ((bf16[1,1,4,192,200]{4,3,1,0,2:T(8,128)(2,1)}), bf16[1,1,4,192,200]{4,3,1,0,2:T(8,128)(2,1)S(1)}, u32[]{:S(2)}, u32[]{:S(2)}) async-start(bf16[1,1,4,192,200]{4,3,1,0,2:T(8,128)(2,1)} %bitcast.52), calls=%async_computation.8 | async-start | bytes 786432 | tf_op jit(solution)/shard_map/all_to_all | solution.py:36
  467.1 134.5 %reduce-scatter.16.cloned.1.call-start = ((), (), s32[]{:S(2)}) async-start(), calls=%async_computation.20 | async-start | bytes 7962624
  493.2 27.6 %copy-start.4 = (f32[1,200,768]{2,1,0:T(8,128)S(1)}, f32[1,200,768]{2,1,0:T(8,128)}, u32[]{:S(2)}) copy-start(f32[1,200,768]{2,1,0:T(8,128)} %param.17) | copy-start | bytes 1843204
  493.2 27.6 %copy-start.44 = (f32[768]{0:T(1024)S(1)}, f32[768]{0:T(1024)}, u32[]{:S(2)}) copy-start(f32[768]{0:T(1024)} %copy-done.43) | copy-start | bytes 9220
  493.2 27.6 %copy-start.46 = (f32[200]{0:T(256)S(1)}, f32[200]{0:T(256)}, u32[]{:S(2)}) copy-start(f32[200]{0:T(256)} %copy-done.45) | copy-start | bytes 2404
  533.5 121.8 %all-reduce.21.cloned.1.call-start = ((), (), s32[]{:S(2)}) async-start(), calls=%async_computation.22 | async-start | bytes 1474560 | tf_op jit(solution)/shard_map/psum | solution.py:340
  561.6 43.7 %copy-start.52 = (f32[768]{0:T(1024)S(1)}, f32[768]{0:T(1024)}, u32[]{:S(2)}) copy-start(f32[768]{0:T(1024)} %get-tuple-element.60) | copy-start | bytes 9220
  561.6 43.7 %copy-start.53 = (f32[768]{0:T(1024)S(1)}, f32[768]{0:T(1024)}, u32[]{:S(2)}) copy-start(f32[768]{0:T(1024)} %get-tuple-element.66) | copy-start | bytes 9220
  561.6 43.7 %copy-start.54 = (f32[768]{0:T(1024)S(1)}, f32[768]{0:T(1024)}, u32[]{:S(2)}) copy-start(f32[768]{0:T(1024)} %get-tuple-element.99) | copy-start | bytes 9220
  603.9 55.3 %copy-start.1 = (bf16[4,512,768]{2,1,0:T(8,128)(2,1)S(1)}, bf16[4,512,768]{2,1,0:T(8,128)(2,1)}, u32[]{:S(2)}) copy-start(bf16[4,512,768]{2,1,0:T(8,128)(2,1)} %param.30) | copy-start | bytes 9437188
  (59 other events, 312.4 us)
Sparse Core Ops, SparseCore 0:
  9.9 36.7 all-gather.5
  65.3 24.3 all-gather.7
  135.1 54.1 all-gather.9
  202.1 53.0 reduce-scatter.9
  312.9 54.7 all-gather.11
  381.5 53.0 reduce-scatter.11
  444.4 34.0 reduce-scatter.17
  481.8 42.4 reduce-scatter.13
  533.7 67.9 reduce-scatter.15
  604.5 43.2 all-reduce.20
where the time goes:
time: 675 us; the launch traced here: 666 us
  waiting for transfers between devices  303 us (45%)
  blocking collectives  142 us (21%)
  matrix products  89.5 us (13%)
  local copies, waits for them, and re-layouts  68.6 us (10%)
  other arithmetic  25.7 us (4%)
  starting transfers between devices  20.9 us (3%)
  between operations  16.6 us (2%)
    all_gather x2, waiting for transfers between devices, gather_rows(): return lax.all_gather(tensor, 'seq', axis=1, tiled=True)  108 us
    reduce_scatter x2, waiting for transfers between devices, sum_partial(): lax.psum_scatter(tensor.astype(jnp.bfloat16), 'seq', scatter_dimension=1,...  106 us
    unnamed x2, blocking collectives  50.7 us
    unnamed x12, waiting for transfers between devices  39.9 us
    all_to_all x2, waiting for transfers between devices, to_heads(): lax.all_to_all(tensor, 'seq', split_axis=2, concat_axis=0, tiled=True)  31.9 us
    all_to_all x2, blocking collectives, to_owners(): return lax.all_to_all(tensor, 'dp', split_axis=0, concat_axis=1, tiled=True)  31 us
    unnamed x180, local copies, waits for them, and re-layouts  29.5 us
    all_to_all x1, blocking collectives, to_tokens(): lax.all_to_all(tensor, 'seq', split_axis=0, concat_axis=1, tiled=True)  26 us
  transfers between devices with their start and end apart: 15, of which 10 were waited for; matrix products, arithmetic and copies ran while one was open for 17% of the time, Pallas kernels for 0%

commit v1 on v0

--- a/solution.py
+++ b/solution.py
@@ -9,6 +9,27 @@
 TOP = 2
 CAP = 14
 epsilon = 1e-06
+
+
+def joined_along(pieces, dim):
+    pieces = jnp.moveaxis(pieces, 0, dim)
+    shape = pieces.shape
+    return pieces.reshape(*shape[:dim], shape[dim] * shape[dim + 1], *shape[dim + 2 :])
+
+
+def grow_blocks(x, axis):
+    length, index = (lax.axis_size(axis), lax.axis_index(axis))
+    parts, bit = (x[None], 1)
+    while bit < length:
+        other = lax.ppermute(parts, axis, [(i, i ^ bit) for i in range(length)])
+        low = index & bit == 0
+        parts = jnp.concatenate([jnp.where(low, parts, other), jnp.where(low, other, parts)])
+        bit *= 2
+    return parts
+
+
+def collect(value, axis, dim):
+    return joined_along(grow_blocks(value, axis), dim)
 
 
 def normalize(values, norm_gain, norm_bias):
@@ -49,7 +70,7 @@
 
 
 def gather_rows(tensor):
-    return lax.all_gather(tensor, "seq", axis=1, tiled=True)
+    return collect(tensor, "seq", 1)
 
 
 def sum_partial(tensor):

time: 675 us -> 735 us (1.089)
  waiting for transfers between devices: 303 us -> 347 us
  other arithmetic: 25.7 us -> 38.5 us
    ppermute x0 -> x4, waiting for transfers between devices: none -> 153 us  [grow_blocks(): other = lax.ppermute(parts, axis, [(i, i ^ bit) for i in range(length)])]
    all_gather x2 -> x0, waiting for transfers between devices: 108 us -> none  [gather_rows(): return lax.all_gather(tensor, 'seq', axis=1, tiled=True)]
    unnamed x180 -> x192, local copies, waits for them, and re-layouts: 29.5 us -> 35.9 us
    unnamed x12 -> x10, waiting for transfers between devices: 39.9 us -> 40 us
  transfers between devices with their start and end apart: 15 -> 17, of which waited for: 10 -> 12; matrix products, arithmetic and copies ran while one was open for 17% -> 16% of each run, Pallas kernels for 0% -> 0%
where the time goes in v1:
time: 735 us; the launch traced here: 726 us
  waiting for transfers between devices  347 us (47%)
  blocking collectives  142 us (19%)
  matrix products  83.5 us (11%)
  local copies, waits for them, and re-layouts  74.7 us (10%)
  other arithmetic  38.5 us (5%)
  starting transfers between devices  23.3 us (3%)
  between operations  16.7 us (2%)
    ppermute x4, waiting for transfers between devices, grow_blocks(): other = lax.ppermute(parts, axis, [(i, i ^ bit) for i in range(length)])  153 us
    reduce_scatter x2, waiting for transfers between devices, sum_partial(): lax.psum_scatter(tensor.astype(jnp.bfloat16), 'seq', scatter_dimension=1,...  106 us
    unnamed x2, blocking collectives  50.6 us
    unnamed x10, waiting for transfers between devices  40 us
    unnamed x192, local copies, waits for them, and re-layouts  35.9 us
    all_to_all x2, waiting for transfers between devices, to_heads(): lax.all_to_all(tensor, 'seq', split_axis=2, concat_axis=0, tiled=True)  32.1 us
    all_to_all x2, blocking collectives, to_owners(): return lax.all_to_all(tensor, 'dp', split_axis=0, concat_axis=1, tiled=True)  31.4 us
    all_to_all x1, blocking collectives, to_tokens(): lax.all_to_all(tensor, 'seq', split_axis=0, concat_axis=1, tiled=True)  25.9 us
  transfers between devices with their start and end apart: 17, of which 12 were waited for; matrix products, arithmetic and copies ran while one was open for 16% of the time, Pallas kernels for 0%

profile of v1, /device:TPU:0, one launch (start us, length us, event | category | flops | bytes accessed | tf_op | source)
XLA Modules:
  0.0 726.0 jit_solution(15400388799871182722)
XLA Ops:
  15.9 26.9 %all-reduce.16 = (bf16[768]{0:T(1024)(128)(2,1)S(1)}, bf16[768]{0:T(1024)(128)(2,1)S(1)}, bf16[768]{0:T(1024)(128)(2,1)S(1)}, bf16[768]{0:T(1024)(128)(2,1)S(1)}...) all-reduce(bf16[768]{0:T(1024)(128)(2,1)S(1)} %dynamic-update-slice, ...), channel_id=1, replica_groups=mesh['dp'=8,'seq'=4] {'dp'}, use_global_device_ids=true, to_apply=%add.4 | all-reduce | flops 5376 | bytes 21504
  46.7 4.1 fusion.10
  58.0 4.6 all-to-all-start
  65.8 25.9 %all-to-all-done = bf16[1,3,4,192,200]{4,3,1,0,2:T(8,128)(2,1)} async-done(((bf16[1,3,4,192,200]{4,3,1,0,2:T(8,128)(2,1)}), bf16[1,3,4,192,200]{4,3,1,0,2:T(8,128)(2,1)}, u32[]{:S(2)}, u32[]{:S(2)}) %all-to-all-start) | async-done | bytes 921632 | tf_op jit(solution)/shard_map/all_to_all | solution.py:57
  95.7 4.3 convolution_convert_fusion.3
  108.2 6.5 all-to-all-done.1
  118.6 15.2 %all_to_all.105 = bf16[32,14,768]{2,1,0:T(8,128)(2,1)S(1)} all-to-all(bf16[32,14,768]{2,1,0:T(8,128)(2,1)S(1)} %copy.103), channel_id=1, replica_groups=mesh['dp'=8,'seq'=4] {'dp'}, dimensions={0} | all-to-all | bytes 1376256 | tf_op jit(solution)/shard_map/all_to_all | solution.py:65
  135.0 16.9 %collective-permute-done = bf16[1,4,112,768]{3,1,2,0:T(4,128)(2,1)} collective-permute-done((bf16[1,4,112,768]{3,1,2,0:T(4,128)(2,1)}, bf16[1,4,112,768]{3,1,2,0:T(4,128)(2,1)}, u32[]{:S(2)}, u32[]{:S(2)}) %collective-permute-start) | collective-permute-done | bytes 688160 | tf_op jit(solution)/shard_map/ppermute | solution.py:24
  156.6 60.9 %collective-permute-done.1 = bf16[2,4,112,768]{3,1,2,0:T(4,128)(2,1)} collective-permute-done((bf16[2,4,112,768]{3,1,2,0:T(4,128)(2,1)}, bf16[2,4,112,768]{3,1,2,0:T(4,128)(2,1)}, u32[]{:S(2)}, u32[]{:S(2)}) %collective-permute-start.1) | collective-permute-done | bytes 1376288 | tf_op jit(solution)/shard_map/ppermute | solution.py:24
  235.2 52.9 %reduce-scatter.10.cloned.1.call-done = bf16[4,112,768]{2,1,0:T(8,128)(2,1)} async-done(((bf16[4,448,768]{2,1,0:T(8,128)(2,1)}), bf16[4,112,768]{2,1,0:T(8,128)(2,1)}) %reduce-scatter.10.cloned.1.call-update) | async-done | bytes 688144 | tf_op jit(solution)/shard_map/reduce_scatter | solution.py:77
  290.4 4.2 all-to-all-start.3
  294.7 14.8 %all-gather = bf16[8,96,32]{1,2,0:T(8,128)(2,1)S(1)} all-gather(bf16[1,96,32]{1,2,0:T(8,128)(2,1)} %bitcast.320), channel_id=1, replica_groups=mesh['dp'=8,'seq'=4] {'dp'}, dimensions={0}, use_global_device_ids=true | all-gather | bytes 55296 | tf_op jit(solution)/shard_map/all_gather | solution.py:170
  328.4 16.2 %all_to_all.106 = bf16[32,14,768]{2,1,0:T(8,128)(2,1)S(1)} all-to-all(bf16[32,14,768]{2,1,0:T(8,128)(2,1)} %convert_element_type.299), channel_id=1, replica_groups=mesh['dp'=8,'seq'=4] {'dp'}, dimensions={0} | all-to-all | bytes 1376256 | tf_op jit(solution)/shard_map/all_to_all | solution.py:65
  345.7 16.0 %collective-permute-done.2 = bf16[1,4,112,768]{3,1,2,0:T(4,128)(2,1)S(1)} collective-permute-done((bf16[1,4,112,768]{3,1,2,0:T(4,128)(2,1)S(1)}, bf16[1,4,112,768]{3,1,2,0:T(4,128)(2,1)S(1)}, u32[]{:S(2)}, u32[]{:S(2)}) %collective-permute-start.2) | collective-permute-done | bytes 688160 | tf_op jit(solution)/shard_map/ppermute | solution.py:24
  364.9 58.8 %collective-permute-done.3 = bf16[2,4,112,768]{3,1,2,0:T(4,128)(2,1)S(1)} collective-permute-done((bf16[2,4,112,768]{3,1,2,0:T(4,128)(2,1)S(1)}, bf16[2,4,112,768]{3,1,2,0:T(4,128)(2,1)S(1)}, u32[]{:S(2)}, u32[]{:S(2)}) %collective-permute-start.3) | collective-permute-done | bytes 1376288 | tf_op jit(solution)/shard_map/ppermute | solution.py:24
  430.3 4.0 multiply_convert_fusion
  440.9 53.3 %reduce-scatter.12.cloned.1.call-done = bf16[4,112,768]{2,1,0:T(8,128)(2,1)} async-done(((bf16[4,448,768]{2,1,0:T(8,128)(2,1)}), bf16[4,112,768]{2,1,0:T(8,128)(2,1)}) %reduce-scatter.12.cloned.1.call-update) | async-done | bytes 688144 | tf_op jit(solution)/shard_map/reduce_scatter | solution.py:77
  502.9 8.6 %all-to-all-done.5 = bf16[4,112,768]{2,0,1:T(4,128)(2,1)S(1)} async-done(((bf16[4,112,768]{2,0,1:T(4,128)(2,1)}), bf16[4,112,768]{2,0,1:T(4,128)(2,1)S(1)}, u32[]{:S(2)}, u32[]{:S(2)}) %all-to-all-start.5) | async-done | bytes 688160 | tf_op jit(solution)/shard_map/all_to_all | solution.py:69
  529.6 6.3 all-to-all-done.6
  536.6 4.3 convolution_convert_fusion.2
  542.6 4.0 fusion.33
  546.5 4.3 fusion.30
  552.9 25.9 %all_to_all.107 = bf16[4,576,200]{1,2,0:T(8,128)(2,1)} all-to-all(bf16[4,576,200]{1,2,0:T(8,128)(2,1)S(1)} %copy.119), channel_id=1, replica_groups=mesh['dp'=8,'seq'=4] {'seq'}, dimensions={0} | all-to-all | bytes 1843200 | tf_op jit(solution)/shard_map/all_to_all | solution.py:61
  585.0 8.0 %copy.133 = f32[768,2304]{1,0:T(8,128)} copy(f32[768,2304]{0,1:T(8,128)} %bitcast.267) | data formatting | bytes 14155776
  593.9 5.9 copy.121
  600.8 6.7 fusion.132
  607.5 4.6 fusion.133
  612.1 4.6 fusion.134
  617.2 3.8 fusion.43
  622.7 38.5 %reduce-scatter.16.cloned.1.call-done = f32[96,2304]{1,0:T(8,128)} async-done(((f32[768,2304]{1,0:T(8,128)}), f32[96,2304]{1,0:T(8,128)}) %reduce-scatter.16.cloned.1.call-update) | async-done | bytes 884752
  664.9 23.7 %all-reduce.15 = (bf16[768]{0:T(1024)(128)(2,1)S(1)}, bf16[768]{0:T(1024)(128)(2,1)S(1)}, bf16[768]{0:T(1024)(128)(2,1)S(1)}, bf16[768]{0:T(1024)(128)(2,1)S(1)}...) all-reduce(f32[768]{0:T(1024)S(1)} %get-tuple-element.62, ...), channel_id=4, replica_groups=mesh['dp'=8,'seq'=4] {'dp'}, use_global_device_ids=true, to_apply=%region_23.24.clone | all-reduce | flops 5376 | bytes 32256
  689.1 19.3 %all-reduce.17 = (bf16[96]{0:T(256)(128)(2,1)S(1)}, bf16[96]{0:T(256)(128)(2,1)S(1)}, bf16[96]{0:T(256)(128)(2,1)S(1)}, bf16[96]{0:T(256)(128)(2,1)S(1)}, bf16[9...) all-reduce(bf16[96]{0:T(256)(128)(2,1)S(1)} %dynamic-slice.34, ...), channel_id=1, replica_groups=mesh['dp'=8,'seq'=4] {'seq'}, use_global_device_ids=true, to_apply=%region_24.25 | all-reduce | flops 3744 | bytes 14976 | tf_op jit(solution)/shard_map/psum | solution.py:359
  (327 shorter events, 155.5 us)
Async XLA Ops:
  7.2 224.9 %copy-start = (bf16[4,512,768]{2,1,0:T(8,128)(2,1)S(1)}, bf16[4,512,768]{2,1,0:T(8,128)(2,1)}, u32[]{:S(2)}) copy-start(bf16[4,512,768]{2,1,0:T(8,128)(2,1)} %param.30) | copy-start | bytes 9437188
  7.2 39.5 %all-gather.4.cloned.1.call-start = ((), (), s32[]{:S(2)}) async-start(), calls=%async_computation.13 | async-start | bytes 3981312 | tf_op jit(solution)/shard_map/all_gather | solution.py:163
  58.0 33.6 %all-to-all-start = ((bf16[1,3,4,192,200]{4,3,1,0,2:T(8,128)(2,1)}), bf16[1,3,4,192,200]{4,3,1,0,2:T(8,128)(2,1)}, u32[]{:S(2)}, u32[]{:S(2)}) async-start(bf16[1,3,4,192,200]{4,3,1,0,2:T(8,128)(2,1)} %copy.97), calls=%async_computation | async-start | bytes 2359296 | tf_op jit(solution)/shard_map/all_to_all | solution.py:57
  62.6 45.6 %all-gather.6.cloned.1.call-start = ((), (), s32[]{:S(2)}) async-start(), calls=%async_computation.14 | async-start | bytes 1327104 | tf_op jit(solution)/shard_map/all_gather | solution.py:166
  64.0 31.7 %copy-start.78 = (f32[4,200]{1,0:T(4,128)}, f32[4,200]{1,0:T(4,128)S(1)}, u32[]{:S(2)}) copy-start(f32[4,200]{1,0:T(4,128)S(1)} %convert_element_type.280) | copy-start | bytes 9604
  100.0 14.7 %all-to-all-start.1 = ((bf16[4,192,200]{2,1,0:T(8,128)(2,1)}), bf16[4,192,200]{2,1,0:T(8,128)(2,1)S(1)}, u32[]{:S(2)}, u32[]{:S(2)}) async-start(bf16[4,192,200]{2,1,0:T(8,128)(2,1)} %bitcast.304), calls=%async_computation.1 | async-start | bytes 786432 | tf_op jit(solution)/shard_map/all_to_all | solution.py:61
  103.5 184.6 %reduce-scatter.10.cloned.1.call-start = ((), (), s32[]{:S(2)}) async-start(), calls=%async_computation.15 | async-start | bytes 3440640 | tf_op jit(solution)/shard_map/reduce_scatter | solution.py:77
  135.0 16.9 %collective-permute-start = (bf16[1,4,112,768]{3,1,2,0:T(4,128)(2,1)}, bf16[1,4,112,768]{3,1,2,0:T(4,128)(2,1)}, u32[]{:S(2)}, u32[]{:S(2)}) collective-permute-start(bf16[1,4,112,768]{3,1,2,0:T(4,128)(2,1)} %bitcast.31), channel_id=1, source_target_pairs={{0,1},{1,0},{2,3},{3,2},{4,5},{5,4},{6,7},{7,6},{8,9},{9,8},{10,11... | collective-permute-start | bytes 2064392 | tf_op jit(solution)/shard_map/ppermute | solution.py:24
  156.3 61.2 %collective-permute-start.1 = (bf16[2,4,112,768]{3,1,2,0:T(4,128)(2,1)}, bf16[2,4,112,768]{3,1,2,0:T(4,128)(2,1)}, u32[]{:S(2)}, u32[]{:S(2)}) collective-permute-start(bf16[2,4,112,768]{3,1,2,0:T(4,128)(2,1)} %pad_maximum_fusion), channel_id=1, source_target_pairs={{0,2},{1,3},{2,0},{3,1},{4,6},{5,7},{6,4},{7,5},{8,10},{9,11},{10,... | collective-permute-start | bytes 4128776 | tf_op jit(solution)/shard_map/ppermute | solution.py:24
  290.4 24.3 %all-to-all-start.3 = ((bf16[4,112,768]{2,0,1:T(4,128)(2,1)}), bf16[4,112,768]{2,0,1:T(4,128)(2,1)}, u32[]{:S(2)}, u32[]{:S(2)}) async-start(bf16[4,112,768]{2,0,1:T(4,128)(2,1)} %copy.106), calls=%async_computation.4 | async-start | bytes 1376256 | tf_op jit(solution)/shard_map/all_to_all | solution.py:69
  294.6 199.5 %reduce-scatter.12.cloned.1.call-start = ((), (), s32[]{:S(2)}) async-start(), calls=%async_computation.16 | async-start | bytes 3440640 | tf_op jit(solution)/shard_map/reduce_scatter | solution.py:77
  345.0 16.7 %collective-permute-start.2 = (bf16[1,4,112,768]{3,1,2,0:T(4,128)(2,1)S(1)}, bf16[1,4,112,768]{3,1,2,0:T(4,128)(2,1)S(1)}, u32[]{:S(2)}, u32[]{:S(2)}) collective-permute-start(bf16[1,4,112,768]{3,1,2,0:T(4,128)(2,1)S(1)} %bitcast.288), channel_id=1, source_target_pairs={{0,1},{1,0},{2,3},{3,2},{4,5},{5,4},{6,7},{7,6},{8,9},{9,8},{10,11... | collective-permute-start | bytes 2064392 | tf_op jit(solution)/shard_map/ppermute | solution.py:24
  362.7 60.9 %collective-permute-start.3 = (bf16[2,4,112,768]{3,1,2,0:T(4,128)(2,1)S(1)}, bf16[2,4,112,768]{3,1,2,0:T(4,128)(2,1)S(1)}, u32[]{:S(2)}, u32[]{:S(2)}) collective-permute-start(bf16[2,4,112,768]{3,1,2,0:T(4,128)(2,1)S(1)} %pad_maximum_fusion.1), channel_id=1, source_target_pairs={{0,2},{1,3},{2,0},{3,1},{4,6},{5,7},{6,4},{7,5},{8,10},{9,11},{10,... | collective-permute-start | bytes 4128776 | tf_op jit(solution)/shard_map/ppermute | solution.py:24
  440.8 59.4 %copy-start.41 = (f32[1,200,2,32]{1,3,2,0:T(8,128)S(1)}, f32[1,200,2,32]{1,3,2,0:T(8,128)}, u32[]{:S(2)}) copy-start(f32[1,200,2,32]{1,3,2,0:T(8,128)} %convert_convert_fusion) | copy-start | bytes 153604
  440.8 59.4 %copy-start.45 = (f32[200,32]{0,1:T(8,128)S(1)}, f32[200,32]{0,1:T(8,128)}, u32[]{:S(2)}) copy-start(f32[200,32]{0,1:T(8,128)} %get-tuple-element.125) | copy-start | bytes 76804
  440.8 59.4 %copy-start.71 = (f32[200]{0:T(256)S(1)}, f32[200]{0:T(256)}, u32[]{:S(2)}) copy-start(f32[200]{0:T(256)} %get-tuple-element.124) | copy-start | bytes 2404
  440.8 59.4 %copy-start.73 = (f32[200]{0:T(256)S(1)}, f32[200]{0:T(256)}, u32[]{:S(2)}) copy-start(f32[200]{0:T(256)} %copy-done.72) | copy-start | bytes 2404
  440.8 59.4 %copy-start.75 = (f32[200]{0:T(256)S(1)}, f32[200]{0:T(256)}, u32[]{:S(2)}) copy-start(f32[200]{0:T(256)} %copy-done.74) | copy-start | bytes 2404
  440.8 59.4 %copy-start.80 = (f32[200]{0:T(256)S(1)}, f32[200]{0:T(256)}, u32[]{:S(2)}) copy-start(f32[200]{0:T(256)} %get-tuple-element.72) | copy-start | bytes 2404
  440.8 59.5 %copy-start.32 = (bf16[1,200,768]{2,1,0:T(8,128)(2,1)S(1)}, bf16[1,200,768]{2,1,0:T(8,128)(2,1)}, u32[]{:S(2)}) copy-start(bf16[1,200,768]{2,1,0:T(8,128)(2,1)} %copy-done.31) | copy-start | bytes 921604
  440.8 61.0 %copy-start.42 = (bf16[768,32]{0,1:T(8,128)(2,1)S(1)}, bf16[768,32]{0,1:T(8,128)(2,1)}, u32[]{:S(2)}) copy-start(bf16[768,32]{0,1:T(8,128)(2,1)} %reshape.685) | copy-start | bytes 147460
  496.4 15.1 %all-to-all-start.5 = ((bf16[4,112,768]{2,0,1:T(4,128)(2,1)}), bf16[4,112,768]{2,0,1:T(4,128)(2,1)S(1)}, u32[]{:S(2)}, u32[]{:S(2)}) async-start(bf16[4,112,768]{2,0,1:T(4,128)(2,1)} %copy.110), calls=%async_computation.7 | async-start | bytes 1376256 | tf_op jit(solution)/shard_map/all_to_all | solution.py:69
  500.1 99.8 %reduce-scatter.18.cloned.1.call-start = ((), (), s32[]{:S(2)}) async-start(), calls=%async_computation.19 | async-start | bytes 442368
  501.4 119.7 %reduce-scatter.14.cloned.1.call-start = ((), (), s32[]{:S(2)}) async-start(), calls=%async_computation.17 | async-start | bytes 2654208 | tf_op jit(solution)/shard_map/reduce_scatter | solution.py:341
  523.2 12.6 %all-to-all-start.6 = ((bf16[1,1,4,192,200]{4,3,1,0,2:T(8,128)(2,1)}), bf16[1,1,4,192,200]{4,3,1,0,2:T(8,128)(2,1)S(1)}, u32[]{:S(2)}, u32[]{:S(2)}) async-start(bf16[1,1,4,192,200]{4,3,1,0,2:T(8,128)(2,1)} %bitcast.58), calls=%async_computation.8 | async-start | bytes 786432 | tf_op jit(solution)/shard_map/all_to_all | solution.py:57
  526.6 134.6 %reduce-scatter.16.cloned.1.call-start = ((), (), s32[]{:S(2)}) async-start(), calls=%async_computation.18 | async-start | bytes 7962624
  552.9 27.5 %copy-start.6 = (f32[1,200,768]{2,1,0:T(8,128)S(1)}, f32[1,200,768]{2,1,0:T(8,128)}, u32[]{:S(2)}) copy-start(f32[1,200,768]{2,1,0:T(8,128)} %param.17) | copy-start | bytes 1843204
  593.1 122.1 %all-reduce.21.cloned.1.call-start = ((), (), s32[]{:S(2)}) async-start(), calls=%async_computation.20 | async-start | bytes 1474560 | tf_op jit(solution)/shard_map/psum | solution.py:361
  621.0 43.8 %copy-start.57 = (f32[768]{0:T(1024)S(1)}, f32[768]{0:T(1024)}, u32[]{:S(2)}) copy-start(f32[768]{0:T(1024)} %get-tuple-element.60) | copy-start | bytes 9220
  621.0 43.8 %copy-start.58 = (f32[768]{0:T(1024)S(1)}, f32[768]{0:T(1024)}, u32[]{:S(2)}) copy-start(f32[768]{0:T(1024)} %get-tuple-element.66) | copy-start | bytes 9220
  621.0 43.8 %copy-start.59 = (f32[768]{0:T(1024)S(1)}, f32[768]{0:T(1024)}, u32[]{:S(2)}) copy-start(f32[768]{0:T(1024)} %get-tuple-element.99) | copy-start | bytes 9220
  663.5 55.5 %copy-start.1 = (bf16[4,512,768]{2,1,0:T(8,128)(2,1)S(1)}, bf16[4,512,768]{2,1,0:T(8,128)(2,1)}, u32[]{:S(2)}) copy-start(bf16[4,512,768]{2,1,0:T(8,128)(2,1)} %param.30) | copy-start | bytes 9437188
  (67 other events, 379.6 us)
Sparse Core Ops, SparseCore 0:
  9.9 36.7 all-gather.3
  65.3 24.3 all-gather.5
  235.3 52.7 reduce-scatter.9
  441.0 53.1 reduce-scatter.11
  503.7 34.0 reduce-scatter.17
  541.0 42.3 reduce-scatter.13
  593.2 67.9 reduce-scatter.15
  664.2 43.1 all-reduce.20
